TPU v7x, 32 devices: a whole 2x2x4 slice. The times are simulated.
32 devices in a mesh: grp: 2 (over x), probe: 8 (over z, y), beam: 2 (over core).
Axes of the slice: x: 2, y: 2, z: 4, core: 2. Of those that a mesh axis runs over, the one named last changes fastest.
Arguments:
- smatrix: bfloat16 [8192, 8, 512], P(('grp', 'beam'), 'probe'), parts along dimension 0, may hold values from -0.09375 to 0.09375
- aperture: float32 [4096], P('beam'), may hold values from 0.5 to 1.5
- aberration: float32 [4096], P('beam'), may hold values from -3.140625 to 3.140625
- beam_k: int32 [2, 4096], P(None, 'beam'), may hold values from -32 to 31, as said below
- probe_pos: int32 [2, 2048], P(None, 'probe'), may hold values from 0 to 1023
- patches: bfloat16 [128, 512], P(('grp', 'probe')), parts along dimension 0, may hold values from -6 to 6
- patch_col: int32 [128], P('grp'), parts along dimension 0, may hold values from 0 to 7, never falling along the last dimension, each value on 1 to 32 neighbouring positions
Outputs:
- ionization: float32 [16, 2048], P('grp', ('probe', 'beam')), parts along dimension 0
There are 2 independent parts, one for each index of `grp`. A program takes and returns all parts, laid end to end along the dimension named above; an argument that names none is the same for every part. Nothing has to cross between parts.
Inputs may be any that keep to these rules, and one draw needn't show every extreme that they name: `patch_col`: patches are ordered by atom column; each of the 8 columns has 1 to 32 patches, and some column has exactly 32. `beam_k`: no two beams have the same pair of indices.
All inputs are finite; a program needn't handle non-finite values.
Results may differ from a plain program's by a relative error of at most 0.005.
Values may be sent and summed in bfloat16 or wider, within the bound.
A program may use at most 128 MiB of HBM per device.

v0:
```python
import math
import jax
import jax.numpy as jnp
from jax import lax
from jax.sharding import PartitionSpec as P

PSIDE = 16
GRID = 1024


def coefficients(beam_k, aperture, aberration, positions):
    turn_count = jnp.mod(
        positions[0][:, None] * beam_k[0][None, :] + positions[1][:, None] * beam_k[1][None, :],
        GRID,
    )
    phase_angle = aberration[None, :] + 2.0 * math.pi / GRID * turn_count.astype(jnp.float32)
    real_coef = (aperture[None, :] * jnp.cos(phase_angle)).astype(jnp.bfloat16)
    imag_coef = (-(aperture[None, :] * jnp.sin(phase_angle))).astype(jnp.bfloat16)
    return (real_coef, imag_coef)


def detector(edge_count):
    half_side = edge_count // 2
    pixel_index = jnp.arange(edge_count * edge_count, dtype=jnp.int32)
    mode_index = jnp.arange(edge_count * half_side, dtype=jnp.int32)
    row_off = pixel_index // edge_count
    col_off = pixel_index % edge_count
    freq_first = mode_index // half_side - half_side
    freq_second = mode_index % half_side - edge_count // 4
    turn_count = jnp.mod(
        row_off[:, None] * freq_first[None, :] + col_off[:, None] * freq_second[None, :], edge_count
    )
    angle_value = 2.0 * math.pi / edge_count * turn_count.astype(jnp.float32)
    real_part = jnp.cos(angle_value)
    imag_part = -jnp.sin(angle_value)
    upper_rows = jnp.concatenate([real_part, imag_part], axis=1)
    lower_rows = jnp.concatenate([-imag_part, real_part], axis=1)
    return jnp.concatenate([upper_rows, lower_rows], axis=0).astype(jnp.bfloat16)


def patch_energy(picked, pot_rows, det_table):
    half_width = pot_rows.shape[-1] // 2
    psi_re = picked[..., :half_width].astype(jnp.float32)
    psi_im = picked[..., half_width:].astype(jnp.float32)
    pot_re = pot_rows[:, :half_width].astype(jnp.float32)
    pot_im = pot_rows[:, half_width:].astype(jnp.float32)
    wave_out = jnp.concatenate(
        [psi_re * pot_re - psi_im * pot_im, psi_re * pot_im + psi_im * pot_re], axis=-1
    ).astype(jnp.bfloat16)
    projected = jnp.einsum("rjx,xq->rjq", wave_out, det_table, preferred_element_type=jnp.float32)
    return jnp.sum(projected * projected, axis=-1) / float(half_width * (det_table.shape[1] // 2))


def combine(beam_terms):
    half_width = beam_terms.shape[-1] // 2
    return jnp.concatenate(
        [
            beam_terms[0, ..., :half_width] - beam_terms[1, ..., half_width:],
            beam_terms[0, ..., half_width:] + beam_terms[1, ..., :half_width],
        ],
        axis=-1,
    )


def spread_patches(psi, all_patches, patch_col, det_table):
    patch_total = all_patches.shape[0]
    group_size = math.gcd(patch_total, 16)
    column_count = psi.shape[1]
    col_groups = patch_col.reshape(patch_total // group_size, group_size)
    pot_groups = all_patches.reshape(patch_total // group_size, group_size, all_patches.shape[1])
    col_range = jnp.arange(column_count, dtype=jnp.int32)

    def add_block(running, blk_pair):
        col_ids, pot_rows = blk_pair
        picked = jnp.take(psi, col_ids, axis=1)
        energy = patch_energy(picked, pot_rows, det_table)
        onehot = (col_ids[:, None] == col_range[None, :]).astype(jnp.float32)
        return (
            running + jnp.einsum("rj,jc->cr", energy, onehot, precision=lax.Precision.HIGHEST),
            None,
        )

    running, _ = lax.scan(
        add_block, jnp.zeros((column_count, psi.shape[0]), jnp.float32), (col_groups, pot_groups)
    )
    return running


def apply_patches(psi_own, all_patches, patch_col, det_table):
    traded = lax.all_to_all(psi_own, "probe", split_axis=0, concat_axis=2, tiled=True)
    return spread_patches(traded[0], all_patches, patch_col, det_table)


def shards(smatrix, aperture, aberration, beam_k, probe_pos, patches, patch_col):
    probe_count = lax.axis_size("probe")
    beam_count = lax.axis_size("beam")
    all_patches = lax.all_gather(patches, "probe", axis=0, tiled=True)
    det_table = detector(PSIDE)
    col_dev = smatrix.shape[1]
    width_two = smatrix.shape[2]
    full_matrix, full_aperture, full_aberration, full_k = (
        lax.all_gather(smatrix, "beam", axis=0, tiled=True),
        lax.all_gather(aperture.astype(jnp.bfloat16), "beam", axis=0, tiled=True).astype(
            aperture.dtype
        ),
        lax.all_gather(aberration.astype(jnp.bfloat16), "beam", axis=0, tiled=True).astype(
            aberration.dtype
        ),
        lax.all_gather(beam_k, "beam", axis=1, tiled=True),
    )
    all_pos = lax.all_gather(probe_pos, "probe", axis=1, tiled=True)
    probe_total = all_pos.shape[1]
    half_probes = probe_total // (beam_count * probe_count)
    split_pos = all_pos.reshape(2, probe_count, beam_count, half_probes)
    mine = lax.dynamic_slice_in_dim(split_pos, lax.axis_index("beam"), 1, 2).reshape(
        2, probe_count * half_probes
    )
    row_total = probe_count * half_probes
    block_rows = math.gcd(row_total, 512)
    pos_blocks = mine.reshape(2, row_total // block_rows, block_rows).transpose(1, 0, 2)

    def whole_block(positions):
        real_coef, imag_coef = coefficients(full_k, full_aperture, full_aberration, positions)
        beam_terms = jnp.einsum(
            "kpb,bcx->kpcx",
            jnp.stack([real_coef, imag_coef]),
            full_matrix,
            preferred_element_type=jnp.float32,
        )
        return combine(beam_terms).astype(jnp.bfloat16)

    psi_own = lax.map(whole_block, pos_blocks).reshape(probe_count, half_probes, col_dev, width_two)
    return apply_patches(psi_own, all_patches, patch_col, det_table)


def solution(mesh):
    placed = (
        P(("grp", "beam"), "probe", None),
        P("beam"),
        P("beam"),
        P(None, "beam"),
        P(None, "probe"),
        P(("grp", "probe"), None),
        P("grp"),
    )
    return jax.shard_map(
        shards, mesh=mesh, in_specs=placed, out_specs=P("grp", ("probe", "beam")), check_vma=False
    )
```

profile of v0, /device:TPU:0, one launch (start us, length us, event | category | flops | bytes accessed | tf_op | source)
XLA Modules:
  0.0 199.8 jit_solution(7711247507291517825)
XLA Ops:
  6.5 0.0 copy-start.3
  6.5 0.0 copy-start.4
  6.5 0.0 copy-start.5
  6.5 0.0 all-gather.2.cloned.1.call-start
  6.6 4.0 %copy.15 = bf16[2048,1,512]{0,2,1:T(8,128)(2,1)} copy(bf16[2048,1,512]{2,0,1:T(8,128)(2,1)} %param.11) | data formatting | bytes 4194304 | tf_op args[0]
  10.6 0.0 all-gather.2.cloned.1.call-update
  10.6 0.0 copy-done.3
  10.6 2.0 all_gather.18
  12.6 0.0 copy-done.4
  12.6 1.8 all_gather.19
  14.4 0.0 copy-done.5
  14.4 27.8 %all_gather.20 = s32[2,2048]{1,0:T(2,128)S(1)} all-gather(s32[2,256]{1,0:T(2,128)S(1)} %copy-done.5), channel_id=1, replica_groups=mesh['grp'=2,'probe'=8,'beam'=2] {'probe'}, dimensions={1}, use_global_device_ids=true | all-gather | bytes 18432 | tf_op jit(solution)/shard_map/all_gather | solution.py:111
  42.3 0.0 copy-done.1
  42.3 1.8 all_gather.21
  44.1 0.0 all-gather.2.cloned.1.call-done
  44.2 0.0 copy-start.6
  44.2 0.0 copy-start.2
  44.2 82.0 %while.23 = (s32[]{:T(128)}, bf16[2,512,1,512]{3,1,0,2:T(8,128)(2,1)}, f32[4096]{0:T(1024)S(1)}, f32[4096]{0:T(1024)S(1)}, s32[2,2,512]{2,0,1:T(2,128)S(1)}, /*i...) while((s32[]{:T(128)}, bf16[2,512,1,512]{3,1,0,2:T(8,128)(2,1)}, ...), condition=%wide.region_1.2_spmd, body=%wide.region_0.1_spmd.sunk | while | flops 4346871808 | bytes 45756576 | solution.py:132
  44.3 0.0 copy-start.7
  44.3 35.1 %multiply_convert_fusion.2 = (bf16[1,512,4096]{2,1,0:T(8,128)(2,1)S(1)}, bf16[1,512,4096]{2,1,0:T(8,128)(2,1)S(1)}) fusion(s32[4096]{0:T(1024)S(1)} %bitcast.69, s32[512]{0:T(512)S(1)} %bitcast.72, s32[4096]{0:T(1024)S(1)} %bitcast.68, s32[512]{0:T(512)S(1)} %bitcast.71, f32[4096]{0:T(1024)S(1)} %get-tuple-element.349, f32[4096]{0:T(1024)S(1)} %get-tuple-element.348), kind=kLoop, calls=%fused_computation.14.clone.1 | loop fusion | flops 46137344 | bytes 8458240 | tf_op jit(solution)/shard_map/while/body/eval_jaxpr/convert_element_type | solution.py:17
  79.4 0.0 copy-done.7
  79.4 4.5 %fusion.66 = f32[2,512,1,512]{1,3,0,2:T(8,128)S(1)} fusion(bf16[4096,1,512]{0,2,1:T(8,128)(2,1)S(1)} %copy-done.7, bf16[1,512,4096]{2,1,0:T(8,128)(2,1)S(1)} %get-tuple-element.310, bf16[1,512,4096]{2,1,0:T(8,128)(2,1)S(1)} %get-tuple-element.311), kind=kOutput, calls=%fused_computation.16.clone.1 | convolution fusion | flops 4299161600 | bytes 14680064 | tf_op jit(solution)/shard_map/while/body/eval_jaxpr/kpb,bcx->kpcx/dot_general | solution.py:124
  83.9 0.2 fusion.67
  84.1 0.2 copy.30
  84.4 0.8 constant_dynamic-update-slice_fusion.2
  85.3 0.0 copy-start.7
  85.3 35.1 %multiply_convert_fusion.2 = (bf16[1,512,4096]{2,1,0:T(8,128)(2,1)S(1)}, bf16[1,512,4096]{2,1,0:T(8,128)(2,1)S(1)}) fusion(s32[4096]{0:T(1024)S(1)} %bitcast.69, s32[512]{0:T(512)S(1)} %bitcast.72, s32[4096]{0:T(1024)S(1)} %bitcast.68, s32[512]{0:T(512)S(1)} %bitcast.71, f32[4096]{0:T(1024)S(1)} %get-tuple-element.349, f32[4096]{0:T(1024)S(1)} %get-tuple-element.348), kind=kLoop, calls=%fused_computation.14.clone.1 | loop fusion | flops 46137344 | bytes 8458240 | tf_op jit(solution)/shard_map/while/body/eval_jaxpr/convert_element_type | solution.py:17
  120.4 0.0 copy-done.7
  120.4 4.5 %fusion.66 = f32[2,512,1,512]{1,3,0,2:T(8,128)S(1)} fusion(bf16[4096,1,512]{0,2,1:T(8,128)(2,1)S(1)} %copy-done.7, bf16[1,512,4096]{2,1,0:T(8,128)(2,1)S(1)} %get-tuple-element.310, bf16[1,512,4096]{2,1,0:T(8,128)(2,1)S(1)} %get-tuple-element.311), kind=kOutput, calls=%fused_computation.16.clone.1 | convolution fusion | flops 4299161600 | bytes 14680064 | tf_op jit(solution)/shard_map/while/body/eval_jaxpr/kpb,bcx->kpcx/dot_general | solution.py:124
  124.9 0.2 fusion.67
  125.1 0.2 copy.30
  125.4 0.8 constant_dynamic-update-slice_fusion.2
  126.2 4.0 %all-to-all-start = ((bf16[8,128,1,512]{3,1,2,0:T(8,128)(2,1)}), bf16[8,128,1,512]{3,1,2,0:T(8,128)(2,1)S(1)}, u32[]{:S(2)}, u32[]{:S(2)}) async-start(bf16[8,128,1,512]{3,1,2,0:T(8,128)(2,1)} %bitcast.9), calls=%async_computation | async-start | bytes 2097152 | tf_op jit(solution)/shard_map/all_to_all | solution.py:90
  130.2 0.0 copy-done.6
  130.2 0.1 reshape.547
  130.3 0.0 copy-done.2
  130.3 46.0 %all_gather.23 = bf16[64,512]{1,0:T(8,128)(2,1)S(1)} all-gather(bf16[8,512]{1,0:T(8,128)(2,1)S(1)} %copy-done.2), channel_id=1, replica_groups=mesh['grp'=2,'probe'=8,'beam'=2] {'probe'}, dimensions={0}, use_global_device_ids=true | all-gather | bytes 73728 | tf_op jit(solution)/shard_map/all_gather | solution.py:97
  176.3 0.6 negate_convert_fusion.1
  177.0 0.0 all-to-all-done
  177.0 15.3 %while.24 = (s32[]{:T(128)}, f32[8,128]{1,0:T(8,128)S(1)}, s32[4,16]{1,0:T(4,128)S(1)}, bf16[128,8,512]{2,0,1:T(8,128)(2,1)S(1)}, bf16[4,16,512]{2,1,0:T(8,128)(...) while((s32[]{:T(128)}, f32[8,128]{1,0:T(8,128)S(1)}, s32[4,16]{1,0:T(4,128)S(1)}, ...), condition=%wide.region_4.5_spmd.clone, body=%wide.region_2.4_spmd.clone.sunk | while | flops 548613504 | bytes 15086163 | solution.py:83
  177.1 0.7 gather_fusion
  177.8 1.3 fusion.73
  179.1 0.7 fusion.74
  179.8 0.8 multiply_reduce_fusion.2
  180.6 0.2 convolution_add_fusion.2
  180.8 0.1 slice_convert_fusion.3
  180.9 0.7 gather_fusion
  181.7 1.3 fusion.73
  182.9 0.7 fusion.74
  183.6 0.8 multiply_reduce_fusion.2
  184.4 0.2 convolution_add_fusion.2
  184.7 0.1 slice_convert_fusion.3
  184.8 0.7 gather_fusion
  185.5 1.3 fusion.73
  186.8 0.7 fusion.74
  187.5 0.8 multiply_reduce_fusion.2
  188.3 0.2 convolution_add_fusion.2
  188.5 0.1 slice_convert_fusion.3
  188.6 0.7 gather_fusion
  189.3 1.3 fusion.73
  190.6 0.7 fusion.74
  191.3 0.8 multiply_reduce_fusion.2
  192.1 0.2 convolution_add_fusion.2
  192.3 0.7 copy-done
  (37 shorter events, 0.4 us)
Async XLA Ops:
  6.5 4.1 %copy-start.3 = (f32[2048]{0:T(1024)S(1)}, f32[2048]{0:T(1024)}, u32[]{:S(2)}) copy-start(f32[2048]{0:T(1024)} %param.12) | copy-start | bytes 24580
  6.5 6.1 %copy-start.4 = (f32[2048]{0:T(1024)S(1)}, f32[2048]{0:T(1024)}, u32[]{:S(2)}) copy-start(f32[2048]{0:T(1024)} %param.13) | copy-start | bytes 24580
  6.5 7.9 %copy-start.5 = (s32[2,256]{1,0:T(2,128)S(1)}, s32[2,256]{1,0:T(2,128)}, u32[]{:S(2)}) copy-start(s32[2,256]{1,0:T(2,128)} %param.15) | copy-start | bytes 6148
  6.5 35.8 %copy-start.1 = (s32[2,2048]{1,0:T(2,128)S(1)}, s32[2,2048]{1,0:T(2,128)}, u32[]{:S(2)}) copy-start(s32[2,2048]{1,0:T(2,128)} %param.14) | copy-start | bytes 49156
  6.5 37.6 %all-gather.2.cloned.1.call-start = ((), (), s32[]{:S(2)}) async-start(), calls=%async_computation.1 | async-start | bytes 6291456 | tf_op jit(solution)/shard_map/all_gather | solution.py:102
  44.2 86.0 %copy-start.6 = (s32[64]{0:T(128)S(1)}, s32[64]{0:T(128)}, u32[]{:S(2)}) copy-start(s32[64]{0:T(128)} %param.17) | copy-start | bytes 772
  44.2 86.1 %copy-start.2 = (bf16[8,512]{1,0:T(8,128)(2,1)S(1)}, bf16[8,512]{1,0:T(8,128)(2,1)}, u32[]{:S(2)}) copy-start(bf16[8,512]{1,0:T(8,128)(2,1)} %param.16) | copy-start | bytes 24580
  44.3 35.1 %copy-start.7 = (bf16[4096,1,512]{0,2,1:T(8,128)(2,1)S(1)}, bf16[4096,1,512]{0,2,1:T(8,128)(2,1)}, u32[]{:S(2)}) copy-start(bf16[4096,1,512]{0,2,1:T(8,128)(2,1)} %get-tuple-element.352) | copy-start | bytes 12582916 | tf_op jit(solution)/shard_map/while
  85.3 35.1 %copy-start.7 = (bf16[4096,1,512]{0,2,1:T(8,128)(2,1)S(1)}, bf16[4096,1,512]{0,2,1:T(8,128)(2,1)}, u32[]{:S(2)}) copy-start(bf16[4096,1,512]{0,2,1:T(8,128)(2,1)} %get-tuple-element.352) | copy-start | bytes 12582916 | tf_op jit(solution)/shard_map/while
  126.2 50.8 %all-to-all-start = ((bf16[8,128,1,512]{3,1,2,0:T(8,128)(2,1)}), bf16[8,128,1,512]{3,1,2,0:T(8,128)(2,1)S(1)}, u32[]{:S(2)}, u32[]{:S(2)}) async-start(bf16[8,128,1,512]{3,1,2,0:T(8,128)(2,1)} %bitcast.9), calls=%async_computation | async-start | bytes 2097152 | tf_op jit(solution)/shard_map/all_to_all | solution.py:90
  192.3 0.7 copy-start
Sparse Core Ops, SparseCore 0:
  10.7 16.3 all-gather.1
where the time goes:
time: 200 us
  other arithmetic  79.6 us (40%)
  blocking collectives  79.5 us (40%)
  between operations  13.5 us (7%)
  matrix products  13.1 us (7%)
  local copies, waits for them, and re-layouts  9.73 us (5%)
  starting transfers between devices  4.03 us (2%)
    convert_element_type x2, other arithmetic, coefficients(): real_coef = (aperture[None, :] * jnp.cos(phase_angle)).astype(jnp.bfloat16)  70.2 us
    all_gather x1, blocking collectives, shards(): all_patches = lax.all_gather(patches, 'probe', axis=0, tiled=True)  46 us
    all_gather x1, blocking collectives, shards(): all_pos = lax.all_gather(probe_pos, 'probe', axis=1, tiled=True)  27.8 us
    dot_general x2, matrix products, whole_block(): jnp.einsum('kpb,bcx->kpcx', jnp.stack([real_coef, imag_coef]), full_matri...  9.05 us
    select_n x8, other arithmetic, add_block(): picked = jnp.take(psi, col_ids, axis=1)  5.19 us
    unnamed x15, local copies, waits for them, and re-layouts  4.67 us
  transfers between devices with their start and end apart: 2, of which 0 were waited for; matrix products, arithmetic and copies ran while one was open for 0% of the time, Pallas kernels for 0%

commit v1 on v0

--- a/solution.py
+++ b/solution.py
@@ -87,7 +87,16 @@
 
 
 def apply_patches(psi_own, all_patches, patch_col, det_table):
-    traded = lax.all_to_all(psi_own, "probe", split_axis=0, concat_axis=2, tiled=True)
+    pair_lines = lambda local_values: jnp.concatenate(
+        lax.all_to_all(
+            jnp.stack(jnp.split(local_values, lax.axis_size("probe"), axis=0), axis=0),
+            "probe",
+            0,
+            0,
+        ),
+        axis=2,
+    )
+    traded = pair_lines(psi_own)
     return spread_patches(traded[0], all_patches, patch_col, det_table)
 
 

time: 200 us -> 204 us (1.020)
  local copies, waits for them, and re-layouts: 9.73 us -> 13.4 us
    unnamed x15 -> x22, local copies, waits for them, and re-layouts: 4.67 us -> 9.28 us
where the time goes in v1:
time: 204 us
  other arithmetic  79.5 us (39%)
  blocking collectives  79.5 us (39%)
  between operations  13.5 us (7%)
  local copies, waits for them, and re-layouts  13.4 us (7%)
  matrix products  13.1 us (6%)
  starting transfers between devices  4.03 us (2%)
    convert_element_type x2, other arithmetic, coefficients(): real_coef = (aperture[None, :] * jnp.cos(phase_angle)).astype(jnp.bfloat16)  70.3 us
    all_gather x1, blocking collectives, shards(): all_patches = lax.all_gather(patches, 'probe', axis=0, tiled=True)  46.1 us
    all_gather x1, blocking collectives, shards(): all_pos = lax.all_gather(probe_pos, 'probe', axis=1, tiled=True)  27.9 us
    unnamed x22, local copies, waits for them, and re-layouts  9.28 us
    dot_general x2, matrix products, whole_block(): jnp.einsum('kpb,bcx->kpcx', jnp.stack([real_coef, imag_coef]), full_matri...  9.05 us
    select_n x8, other arithmetic, add_block(): picked = jnp.take(psi, col_ids, axis=1)  5.24 us
  transfers between devices with their start and end apart: 2, of which 0 were waited for; matrix products, arithmetic and copies ran while one was open for 0% of the time, Pallas kernels for 0%

profile of v1, /device:TPU:0, one launch (start us, length us, event | category | flops | bytes accessed | tf_op | source)
XLA Modules:
  0.0 203.8 jit_solution(8432644469660937466)
XLA Ops:
  6.5 0.0 all-gather.2.cloned.1.call-start
  6.6 4.0 %copy.23 = bf16[2048,1,512]{0,2,1:T(8,128)(2,1)} copy(bf16[2048,1,512]{2,0,1:T(8,128)(2,1)} %param.11) | data formatting | bytes 4194304 | tf_op args[0]
  10.6 0.0 all-gather.2.cloned.1.call-update
  10.6 0.0 copy-done.5
  10.6 27.9 %all_gather.20 = s32[2,2048]{1,0:T(2,128)S(1)} all-gather(s32[2,256]{1,0:T(2,128)S(1)} %copy-done.5), channel_id=1, replica_groups=mesh['grp'=2,'probe'=8,'beam'=2] {'probe'}, dimensions={1}, use_global_device_ids=true | all-gather | bytes 18432 | tf_op jit(solution)/shard_map/all_gather | solution.py:120
  38.6 0.0 copy-done.3
  38.6 1.8 all_gather.18
  40.5 0.0 copy-done.4
  40.5 1.8 all_gather.19
  42.3 0.0 copy-done.1
  42.3 1.8 all_gather.21
  44.1 0.0 all-gather.2.cloned.1.call-done
  44.2 80.7 %while.23 = (s32[]{:T(128)}, bf16[2,512,1,512]{3,1,0,2:T(8,128)(2,1)S(1)}, f32[4096]{0:T(1024)S(1)}, f32[4096]{0:T(1024)S(1)}, s32[2,2,512]{2,0,1:T(2,128)S(1)},...) while((s32[]{:T(128)}, ...), condition=%wide.region_1.2_spmd, body=%wide.region_0.1_spmd.sunk | while | flops 4346871808 | bytes 45756568 | solution.py:141
  44.2 0.0 copy-start.7
  44.2 35.1 %multiply_convert_fusion.2 = (bf16[1,512,4096]{2,1,0:T(8,128)(2,1)S(1)}, bf16[1,512,4096]{2,1,0:T(8,128)(2,1)S(1)}) fusion(s32[4096]{0:T(1024)S(1)} %bitcast.97, s32[512]{0:T(512)S(1)} %bitcast.108, s32[4096]{0:T(1024)S(1)} %bitcast.96, s32[512]{0:T(512)S(1)} %bitcast.107, f32[4096]{0:T(1024)S(1)} %get-tuple-element.349, f32[4096]{0:T(1024)S(1)} %get-tuple-element.348), kind=kLoop, calls=%fused_computation.14.clone.1 | loop fusion | flops 46137344 | bytes 8458240 | tf_op jit(solution)/shard_map/while/body/eval_jaxpr/convert_element_type | solution.py:17
  79.4 0.0 copy-done.7
  79.4 4.5 %fusion.74 = f32[2,512,1,512]{1,3,0,2:T(8,128)S(1)} fusion(bf16[4096,1,512]{0,2,1:T(8,128)(2,1)S(1)} %copy-done.7, bf16[1,512,4096]{2,1,0:T(8,128)(2,1)S(1)} %get-tuple-element.310, bf16[1,512,4096]{2,1,0:T(8,128)(2,1)S(1)} %get-tuple-element.311), kind=kOutput, calls=%fused_computation.16.clone.1 | convolution fusion | flops 4299161600 | bytes 14680064 | tf_op jit(solution)/shard_map/while/body/eval_jaxpr/kpb,bcx->kpcx/dot_general | solution.py:133
  83.9 0.2 fusion.75
  84.1 0.2 copy.37
  84.5 0.0 copy-start.7
  84.5 35.1 %multiply_convert_fusion.2 = (bf16[1,512,4096]{2,1,0:T(8,128)(2,1)S(1)}, bf16[1,512,4096]{2,1,0:T(8,128)(2,1)S(1)}) fusion(s32[4096]{0:T(1024)S(1)} %bitcast.97, s32[512]{0:T(512)S(1)} %bitcast.108, s32[4096]{0:T(1024)S(1)} %bitcast.96, s32[512]{0:T(512)S(1)} %bitcast.107, f32[4096]{0:T(1024)S(1)} %get-tuple-element.349, f32[4096]{0:T(1024)S(1)} %get-tuple-element.348), kind=kLoop, calls=%fused_computation.14.clone.1 | loop fusion | flops 46137344 | bytes 8458240 | tf_op jit(solution)/shard_map/while/body/eval_jaxpr/convert_element_type | solution.py:17
  119.6 0.0 copy-done.7
  119.6 4.5 %fusion.74 = f32[2,512,1,512]{1,3,0,2:T(8,128)S(1)} fusion(bf16[4096,1,512]{0,2,1:T(8,128)(2,1)S(1)} %copy-done.7, bf16[1,512,4096]{2,1,0:T(8,128)(2,1)S(1)} %get-tuple-element.310, bf16[1,512,4096]{2,1,0:T(8,128)(2,1)S(1)} %get-tuple-element.311), kind=kOutput, calls=%fused_computation.16.clone.1 | convolution fusion | flops 4299161600 | bytes 14680064 | tf_op jit(solution)/shard_map/while/body/eval_jaxpr/kpb,bcx->kpcx/dot_general | solution.py:133
  124.2 0.2 fusion.75
  124.4 0.2 copy.37
  124.8 0.0 copy-start.6
  124.8 0.0 copy-start.2
  124.9 0.7 fusion.50
  125.5 0.7 fusion.49
  126.2 0.7 fusion.48
  126.8 0.7 fusion.47
  127.5 0.7 fusion.46
  128.1 0.7 fusion.45
  128.8 0.7 fusion.44
  129.5 0.7 fusion.43
  130.1 4.0 %all-to-all-start = ((bf16[8,1,128,1,512]{4,2,3,1,0:T(8,128)(2,1)}), bf16[8,1,128,1,512]{4,2,3,1,0:T(8,128)(2,1)S(1)}, u32[]{:S(2)}, u32[]{:S(2)}) async-start(bf16[8,1,128,1,512]{4,2,3,1,0:T(8,128)(2,1)} %fusion.43), calls=%async_computation | async-start | bytes 2097152 | tf_op jit(solution)/shard_map/all_to_all | solution.py:91
  134.1 0.0 copy-done.6
  134.1 0.1 reshape.549
  134.2 0.0 copy-done.2
  134.2 46.1 %all_gather.23 = bf16[64,512]{1,0:T(8,128)(2,1)S(1)} all-gather(bf16[8,512]{1,0:T(8,128)(2,1)S(1)} %copy-done.2), channel_id=1, replica_groups=mesh['grp'=2,'probe'=8,'beam'=2] {'probe'}, dimensions={0}, use_global_device_ids=true | all-gather | bytes 73728 | tf_op jit(solution)/shard_map/all_gather | solution.py:106
  180.3 0.6 negate_convert_fusion.1
  181.0 0.0 all-to-all-done
  181.0 15.3 %while.24 = (s32[]{:T(128)}, f32[8,128]{1,0:T(8,128)S(1)}, s32[4,16]{1,0:T(4,128)S(1)}, bf16[128,8,512]{2,0,1:T(8,128)(2,1)S(1)}, bf16[4,16,512]{2,1,0:T(8,128)(...) while((s32[]{:T(128)}, f32[8,128]{1,0:T(8,128)S(1)}, s32[4,16]{1,0:T(4,128)S(1)}, ...), condition=%wide.region_4.5_spmd.clone, body=%wide.region_2.4_spmd.clone.sunk | while | flops 548613504 | bytes 15086155 | solution.py:83
  181.0 0.7 gather_fusion
  181.7 1.3 fusion.81
  183.1 0.7 fusion.82
  183.8 0.8 multiply_reduce_fusion.2
  184.6 0.2 convolution_add_fusion.2
  184.9 0.7 gather_fusion
  185.6 1.3 fusion.81
  186.9 0.7 fusion.82
  187.6 0.8 multiply_reduce_fusion.2
  188.4 0.2 convolution_add_fusion.2
  188.7 0.7 gather_fusion
  189.4 1.3 fusion.81
  190.7 0.7 fusion.82
  191.4 0.8 multiply_reduce_fusion.2
  192.2 0.2 convolution_add_fusion.2
  192.5 0.7 gather_fusion
  193.2 1.3 fusion.81
  194.6 0.7 fusion.82
  195.3 0.8 multiply_reduce_fusion.2
  196.1 0.2 convolution_add_fusion.2
  196.3 0.7 copy-done
  (45 shorter events, 0.6 us)
Async XLA Ops:
  6.5 4.1 %copy-start.5 = (s32[2,256]{1,0:T(2,128)S(1)}, s32[2,256]{1,0:T(2,128)}, u32[]{:S(2)}) copy-start(s32[2,256]{1,0:T(2,128)} %param.15) | copy-start | bytes 6148
  6.5 32.1 %copy-start.3 = (f32[2048]{0:T(1024)S(1)}, f32[2048]{0:T(1024)}, u32[]{:S(2)}) copy-start(f32[2048]{0:T(1024)} %param.12) | copy-start | bytes 24580
  6.5 33.9 %copy-start.4 = (f32[2048]{0:T(1024)S(1)}, f32[2048]{0:T(1024)}, u32[]{:S(2)}) copy-start(f32[2048]{0:T(1024)} %param.13) | copy-start | bytes 24580
  6.5 35.8 %copy-start.1 = (s32[2,2048]{1,0:T(2,128)S(1)}, s32[2,2048]{1,0:T(2,128)}, u32[]{:S(2)}) copy-start(s32[2,2048]{1,0:T(2,128)} %param.14) | copy-start | bytes 49156
  6.5 37.6 %all-gather.2.cloned.1.call-start = ((), (), s32[]{:S(2)}) async-start(), calls=%async_computation.1 | async-start | bytes 6291456 | tf_op jit(solution)/shard_map/all_gather | solution.py:111
  44.2 35.2 %copy-start.7 = (bf16[4096,1,512]{0,2,1:T(8,128)(2,1)S(1)}, bf16[4096,1,512]{0,2,1:T(8,128)(2,1)}, u32[]{:S(2)}) copy-start(bf16[4096,1,512]{0,2,1:T(8,128)(2,1)} %get-tuple-element.352) | copy-start | bytes 12582916 | tf_op jit(solution)/shard_map/while
  84.5 35.2 %copy-start.7 = (bf16[4096,1,512]{0,2,1:T(8,128)(2,1)S(1)}, bf16[4096,1,512]{0,2,1:T(8,128)(2,1)}, u32[]{:S(2)}) copy-start(bf16[4096,1,512]{0,2,1:T(8,128)(2,1)} %get-tuple-element.352) | copy-start | bytes 12582916 | tf_op jit(solution)/shard_map/while
  124.8 9.3 %copy-start.6 = (s32[64]{0:T(128)S(1)}, s32[64]{0:T(128)}, u32[]{:S(2)}) copy-start(s32[64]{0:T(128)} %param.17) | copy-start | bytes 772
  124.8 9.4 %copy-start.2 = (bf16[8,512]{1,0:T(8,128)(2,1)S(1)}, bf16[8,512]{1,0:T(8,128)(2,1)}, u32[]{:S(2)}) copy-start(bf16[8,512]{1,0:T(8,128)(2,1)} %param.16) | copy-start | bytes 24580
  130.1 50.9 %all-to-all-start = ((bf16[8,1,128,1,512]{4,2,3,1,0:T(8,128)(2,1)}), bf16[8,1,128,1,512]{4,2,3,1,0:T(8,128)(2,1)S(1)}, u32[]{:S(2)}, u32[]{:S(2)}) async-start(bf16[8,1,128,1,512]{4,2,3,1,0:T(8,128)(2,1)} %fusion.43), calls=%async_computation | async-start | bytes 2097152 | tf_op jit(solution)/shard_map/all_to_all | solution.py:91
  196.3 0.7 copy-start
Sparse Core Ops, SparseCore 0:
  10.7 16.3 all-gather.1
